TPU v7x, 512 devices: a whole 4x4x16 slice. The times are simulated.
512 devices in a mesh: row: 16 (over z), col: 4 (over x_hi, core), layer: 8 (over x_lo, y).
Axes of the slice: x: 4 (x_hi: 2, x_lo: 2; x = x_hi * 2 + x_lo), y: 4, z: 16, core: 2. Of those that a mesh axis runs over, the one named last changes fastest.
Arguments:
- blocks: float32 [4096, 128, 128], P(('row', 'col', 'layer')), may hold values from -0.6 to 0.6
- block_ids: int32 [4096, 2], P(('row', 'col', 'layer')), may hold values from -1 to 1535, as said below
- out_ids: int32 [4096, 2], P(('row', 'col')), may hold values from -1 to 1535, as said below
Outputs:
- products: float32 [4096, 128, 128], P(('row', 'col', 'layer'))
Inputs may be any that keep to these rules, and one draw needn't show every extreme that they name: `block_ids`: each row is the (block row, block column) of one slot, or (-1, -1) for an empty slot. The device at index (r, c, l) of (row, col, layer) holds blocks whose row is r modulo 16 and whose column is c * 8 + l modulo 4 * 8. Each row group r has between 1 and 4 block rows in use, and each column class has exactly 2 block columns in use; a device holds every block where its row group's rows in use meet its class's columns, each once, in no set order, and its other slots are empty. Some 4 + 1 row groups in a row (wrapping around) have 4 rows in use. `out_ids`: the 64 rows for the index pair (r, c) of (row, col) list, in no set order, each pair (i, j) once where i is a block row in use of row group r and j one of row group (r + 4 c + m) modulo 16 for some m < 4; the remaining rows are (-1, -1).
All inputs are finite; a program needn't handle non-finite values.
Results may differ from a plain program's by a relative error of at most 0.0003.
Values sent between devices are 32-bit elements; how exact they have to be, the bound alone decides.
No kernel may reach another device: no remote copies, remote signals or barrier semaphores. Data moves between devices by JAX's collectives and lax.ppermute only.
A program may use at most 64 MiB of HBM per device.

v0:
```python
import jax
import jax.numpy as jnp
from jax import lax
from jax.sharding import PartitionSpec as P

NB = 1536
ROWS_G = 4
HIGH = lax.Precision.HIGHEST


def shifted(value, axis, steps):
    count = lax.axis_size(axis)
    pairs = [(source, (source + steps) % count) for source in range(count)]
    return lax.ppermute(value, axis, pairs)


def arrange(panel_blocks, panel_coords, row_total):
    slot_total = panel_blocks.shape[0]
    width = panel_blocks.shape[1]
    per_row = slot_total // row_total
    row_ids = panel_coords[:, 0]
    col_ids = panel_coords[:, 1]
    slot_range = jnp.arange(slot_total, dtype=jnp.int32)
    sort_key = jnp.where(row_ids >= 0, row_ids * NB + col_ids, 2**30 + slot_range)
    rank_of = jnp.sum((sort_key[None, :] < sort_key[:, None]).astype(jnp.int32), axis=1)
    gather_order = jnp.sum(
        jnp.where(rank_of[None, :] == slot_range[:, None], slot_range[None, :], 0), axis=1
    )
    ordered = jnp.take(panel_blocks, gather_order, axis=0)
    row_heads = jnp.take(row_ids, gather_order)[::per_row]
    shaped = ordered.reshape(row_total, per_row, width, width).transpose(0, 2, 1, 3)
    shaped = shaped.reshape(row_total, width, per_row * width)
    shaped = jnp.where((row_heads >= 0)[:, None, None], shaped, jnp.float32(0.0))
    return (shaped.reshape(row_total * width, per_row * width), row_heads)


def locate(targets, heads):
    hits = (targets[:, None] == heads[None, :]) & (targets[:, None] >= 0)
    found = jnp.any(hits, axis=1)
    head_range = jnp.arange(heads.shape[0], dtype=jnp.int32)
    where_at = jnp.sum(jnp.where(hits, head_range[None, :], 0), axis=1)
    return (where_at, found)


def shards(blocks, block_ids, out_ids):
    row_count = lax.axis_size("row")
    col_count = lax.axis_size("col")
    stride = row_count // col_count
    col_index = lax.axis_index("col")
    width = blocks.shape[1]
    left_blocks, left_coords = (
        lax.all_gather(blocks, "col", axis=0, tiled=True),
        lax.all_gather(block_ids, "col", axis=0, tiled=True),
    )
    base_blocks, base_coords = (left_blocks, left_coords)
    far_blocks, far_coords = (left_blocks, left_coords)
    for offset in range(1, col_count):
        far_blocks, far_coords = shifted((far_blocks, far_coords), "row", row_count - stride)
        chosen = col_index == offset
        base_blocks = jnp.where(chosen, far_blocks, base_blocks)
        base_coords = jnp.where(chosen, far_coords, base_coords)
    block_list = [base_blocks]
    coord_list = [base_coords]
    for offset in range(1, stride):
        far_blocks, far_coords = shifted((block_list[-1], coord_list[-1]), "row", row_count - 1)
        block_list.append(far_blocks)
        coord_list.append(far_coords)
    stack_blocks = jnp.stack(block_list, axis=0)
    stack_coords = jnp.stack(coord_list, axis=0)
    left_dense, left_heads = arrange(left_blocks, left_coords, ROWS_G)
    right_dense, right_heads = jax.vmap(
        lambda stack_piece, coord_piece: arrange(stack_piece, coord_piece, ROWS_G)
    )(stack_blocks, stack_coords)
    right_dense = right_dense.reshape(-1, right_dense.shape[-1])
    right_heads = right_heads.reshape(-1)
    right_total = right_heads.shape[0]
    partial_all = lax.dot_general(
        left_dense,
        right_dense,
        (((1,), (1,)), ((), ())),
        precision=HIGH,
        preferred_element_type=jnp.float32,
    )
    tiled = (
        partial_all.reshape(ROWS_G, width, right_total, width)
        .transpose(0, 2, 1, 3)
        .reshape(ROWS_G * right_total, width, width)
    )
    left_at, left_found = locate(out_ids[:, 0], left_heads)
    right_at, right_found = locate(out_ids[:, 1], right_heads)
    picked = jnp.take(tiled, left_at * right_total + right_at, axis=0)
    picked = jnp.where((left_found & right_found)[:, None, None], picked, jnp.float32(0.0))
    return lax.psum_scatter(picked, "layer", scatter_dimension=0, tiled=True)


def solution(mesh):
    return jax.shard_map(
        shards,
        mesh=mesh,
        in_specs=(
            P(("row", "col", "layer"), None, None),
            P(("row", "col", "layer"), None),
            P(("row", "col"), None),
        ),
        out_specs=P(("row", "col", "layer"), None, None),
        check_vma=False,
    )
```

profile of v0, /device:TPU:1, one launch (start us, length us, event | category | flops | bytes accessed | tf_op | source)
XLA Modules:
  0.0 921.1 jit_solution(10634318678526448864)
XLA Ops:
  7.3 42.2 %all-gather.3.cloned.1.call-done = f32[32,128,128]{2,1,0:T(8,128)} async-done(((f32[8,128,128]{2,1,0:T(8,128)}), f32[32,128,128]{2,1,0:T(8,128)}) %all-gather.3.cloned.1.call-update) | async-done | bytes 2097168 | tf_op jit(solution)/shard_map/all_gather | solution.py:52
  49.5 8.1 collective-permute-start.6
  57.6 283.4 %collective-permute-done.6 = f32[32,128,128]{2,1,0:T(8,128)S(1)} collective-permute-done((f32[32,128,128]{2,1,0:T(8,128)}, f32[32,128,128]{2,1,0:T(8,128)S(1)}, u32[]{:S(2)}, u32[]{:S(2)}) %collective-permute-start.6) | collective-permute-done | bytes 2097184 | tf_op jit(solution)/shard_map/ppermute | solution.py:14
  342.3 9.6 %collective-permute-start.7 = (f32[32,128,128]{2,1,0:T(8,128)S(1)}, f32[32,128,128]{2,1,0:T(8,128)S(1)}, u32[]{:S(2)}, u32[]{:S(2)}) collective-permute-start(f32[32,128,128]{2,1,0:T(8,128)S(1)} %collective-permute-done.6), channel_id=1, source_target_pairs={{0,384},{32,416},{64,448},{96,480},{128,0},{160,32},{192,64},{224,... | collective-permute-start | bytes 6291464 | tf_op jit(solution)/shard_map/ppermute | solution.py:14
  351.9 178.9 %collective-permute-done.7 = f32[32,128,128]{2,1,0:T(8,128)S(1)} collective-permute-done((f32[32,128,128]{2,1,0:T(8,128)S(1)}, f32[32,128,128]{2,1,0:T(8,128)S(1)}, u32[]{:S(2)}, u32[]{:S(2)}) %collective-permute-start.7) | collective-permute-done | bytes 2097184 | tf_op jit(solution)/shard_map/ppermute | solution.py:14
  532.8 68.6 %collective-permute-done.8 = f32[32,128,128]{2,1,0:T(8,128)} collective-permute-done((f32[32,128,128]{2,1,0:T(8,128)S(1)}, f32[32,128,128]{2,1,0:T(8,128)}, u32[]{:S(2)}, u32[]{:S(2)}) %collective-permute-start.8) | collective-permute-done | bytes 2097184 | tf_op jit(solution)/shard_map/ppermute | solution.py:14
  601.4 2.4 select_select_fusion.1
  603.8 1.9 collective-permute-start.9
  605.7 12.6 %all-gather = s32[4,8,2]{1,2,0:T(2,128)S(1)} all-gather(s32[1,8,2]{1,2,0:T(2,128)S(1)} %bitcast.72), channel_id=1, replica_groups=mesh['row'=16,'col'=4,'layer'=8] {'col'}, dimensions={0}, use_global_device_ids=true | all-gather | bytes 320 | tf_op jit(solution)/shard_map/all_gather | solution.py:53
  618.4 6.9 collective-permute-start
  625.7 21.0 %collective-permute-done.9 = f32[32,128,128]{2,1,0:T(8,128)} collective-permute-done((f32[32,128,128]{2,1,0:T(8,128)S(1)}, f32[32,128,128]{2,1,0:T(8,128)}, u32[]{:S(2)}, u32[]{:S(2)}) %collective-permute-start.9) | collective-permute-done | bytes 2097184 | tf_op jit(solution)/shard_map/ppermute | solution.py:14
  646.7 8.3 collective-permute-start.10
  655.7 5.2 collective-permute-done
  663.0 47.3 %collective-permute-done.1 = s32[32,2]{0,1:T(2,128)S(1)} collective-permute-done((s32[32,2]{0,1:T(2,128)S(1)}, s32[32,2]{0,1:T(2,128)S(1)}, u32[]{:S(2)}, u32[]{:S(2)}) %collective-permute-start.1) | collective-permute-done | bytes 288 | tf_op jit(solution)/shard_map/ppermute | solution.py:14
  712.2 6.3 collective-permute-done.2
  718.5 2.2 collective-permute-start.3
  720.7 2.0 collective-permute-done.3
  722.8 3.4 collective-permute-start.4
  727.2 4.5 collective-permute-start.5
  732.4 5.0 collective-permute-start.11
  740.1 2.3 gather_fusion.1
  742.7 2.6 copy.26
  747.0 28.7 %collective-permute-done.11 = f32[32,128,128]{2,1,0:T(8,128)} collective-permute-done((f32[32,128,128]{2,1,0:T(8,128)}, f32[32,128,128]{2,1,0:T(8,128)}, u32[]{:S(2)}, u32[]{:S(2)}) %collective-permute-start.11) | collective-permute-done | bytes 2097184 | tf_op jit(solution)/shard_map/ppermute | solution.py:14
  775.7 5.9 pad_maximum_fusion
  781.6 7.7 gather_fusion.4
  789.2 4.2 select_bitcast_fusion
  793.5 9.7 %copy.27 = f32[4,4,128,8,128]{4,3,2,1,0:T(8,128)} copy(f32[4,4,128,8,128]{4,2,3,1,0:T(8,128)S(1)} %select_bitcast_fusion) | data formatting | bytes 16777216 | tf_op jit(solution)/shard_map/vmap(jit(_where))/select_n | solution.py:33
  803.2 9.3 %reshape.227 = f32[16,128,1024,1]{2,1,0,3:T(8,128)} reshape(f32[4,4,128,8,128]{4,3,2,1,0:T(8,128)} %copy.27) | data formatting | bytes 16777216 | tf_op jit(solution)/shard_map/vmap(jit(_where))/select_n | solution.py:33
  812.5 17.6 %fusion = f32[4,128,16,128]{3,1,2,0:T(8,128)} fusion(f32[16,128,1024,1]{2,1,0,3:T(8,128)} %reshape.227, f32[4,128,1024,1]{2,1,0,3:T(8,128)S(1)} %reshape.226), kind=kOutput, calls=%fused_computation.8 | convolution fusion | flops 12884901888 | bytes 14680064 | tf_op jit(solution)/shard_map/dot_general | solution.py:77
  830.1 4.9 gather_fusion.2
  835.0 4.6 select_select_fusion
  839.7 74.6 %reduce-scatter.2.cloned.1.call-done = f32[8,128,128]{2,1,0:T(8,128)} async-done(((f32[64,128,128]{2,1,0:T(8,128)}), f32[8,128,128]{2,1,0:T(8,128)}) %reduce-scatter.2.cloned.1.call-update) | async-done | bytes 524304 | tf_op jit(solution)/shard_map/reduce_scatter | solution.py:93
  (63 shorter events, 15.6 us)
Async XLA Ops:
  6.5 43.0 %all-gather.3.cloned.1.call-start = ((), (), s32[]{:S(2)}) async-start(), calls=%async_computation.1 | async-start | bytes 2621440 | tf_op jit(solution)/shard_map/all_gather | solution.py:52
  7.3 907.0 %reduce-scatter.2.cloned.1.call-start = ((), (), s32[]{:S(2)}) async-start(), calls=%async_computation.2 | async-start | bytes 4718592 | tf_op jit(solution)/shard_map/reduce_scatter | solution.py:93
  49.5 291.5 %collective-permute-start.6 = (f32[32,128,128]{2,1,0:T(8,128)}, f32[32,128,128]{2,1,0:T(8,128)S(1)}, u32[]{:S(2)}, u32[]{:S(2)}) collective-permute-start(f32[32,128,128]{2,1,0:T(8,128)} %all-gather.3.cloned.1.call-done), channel_id=1, source_target_pairs={{0,384},{32,416},{64,448},{96,480},{128,0},{160,32},{192,64},{224,... | collective-permute-start | bytes 6291464 | tf_op jit(solution)/shard_map/ppermute | solution.py:14
  341.0 1.3 copy-start.1
  342.3 188.5 %collective-permute-start.7 = (f32[32,128,128]{2,1,0:T(8,128)S(1)}, f32[32,128,128]{2,1,0:T(8,128)S(1)}, u32[]{:S(2)}, u32[]{:S(2)}) collective-permute-start(f32[32,128,128]{2,1,0:T(8,128)S(1)} %collective-permute-done.6), channel_id=1, source_target_pairs={{0,384},{32,416},{64,448},{96,480},{128,0},{160,32},{192,64},{224,... | collective-permute-start | bytes 6291464 | tf_op jit(solution)/shard_map/ppermute | solution.py:14
  530.8 1.9 copy-start.2
  530.8 70.6 %collective-permute-start.8 = (f32[32,128,128]{2,1,0:T(8,128)S(1)}, f32[32,128,128]{2,1,0:T(8,128)}, u32[]{:S(2)}, u32[]{:S(2)}) collective-permute-start(f32[32,128,128]{2,1,0:T(8,128)S(1)} %collective-permute-done.7), channel_id=1, source_target_pairs={{0,384},{32,416},{64,448},{96,480},{128,0},{160,32},{192,64},{224,... | collective-permute-start | bytes 6291464 | tf_op jit(solution)/shard_map/ppermute | solution.py:14
  532.8 73.0 %copy-start.4 = (s32[8,2]{0,1:T(2,128)S(1)}, s32[8,2]{0,1:T(2,128)}, u32[]{:S(2)}) copy-start(s32[8,2]{0,1:T(2,128)} %param.4) | copy-start | bytes 196
  532.8 92.9 %copy-start.3 = (s32[64,2]{0,1:T(2,128)S(1)}, s32[64,2]{0,1:T(2,128)}, u32[]{:S(2)}) copy-start(s32[64,2]{0,1:T(2,128)} %param.5) | copy-start | bytes 1540
  603.8 128.6 %copy-start = (f32[32,128,128]{2,1,0:T(8,128)}, f32[32,128,128]{2,1,0:T(8,128)S(1)}, u32[]{:S(2)}) copy-start(f32[32,128,128]{2,1,0:T(8,128)S(1)} %select_select_fusion.1) | copy-start | bytes 6291460
  603.8 42.9 %collective-permute-start.9 = (f32[32,128,128]{2,1,0:T(8,128)S(1)}, f32[32,128,128]{2,1,0:T(8,128)}, u32[]{:S(2)}, u32[]{:S(2)}) collective-permute-start(f32[32,128,128]{2,1,0:T(8,128)S(1)} %select_select_fusion.1), channel_id=1, source_target_pairs={{0,480},{32,0},{64,32},{96,64},{128,96},{160,128},{192,160},{224,1... | collective-permute-start | bytes 6291464 | tf_op jit(solution)/shard_map/ppermute | solution.py:14
  618.4 42.6 %collective-permute-start = (s32[32,2]{0,1:T(2,128)S(1)}, s32[32,2]{0,1:T(2,128)S(1)}, u32[]{:S(2)}, u32[]{:S(2)}) collective-permute-start(s32[32,2]{0,1:T(2,128)S(1)} %reshape.225), channel_id=1, source_target_pairs={{0,384},{32,416},{64,448},{96,480},{128,0},{160,32},{192,64},{224,... | collective-permute-start | bytes 776 | tf_op jit(solution)/shard_map/ppermute | solution.py:14
  646.7 85.7 %collective-permute-start.10 = (f32[32,128,128]{2,1,0:T(8,128)}, f32[32,128,128]{2,1,0:T(8,128)}, u32[]{:S(2)}, u32[]{:S(2)}) collective-permute-start(f32[32,128,128]{2,1,0:T(8,128)} %collective-permute-done.9), channel_id=1, source_target_pairs={{0,480},{32,0},{64,32},{96,64},{128,96},{160,128},{192,160},{224,1... | collective-permute-start | bytes 6291464 | tf_op jit(solution)/shard_map/ppermute | solution.py:14
  661.0 49.3 %collective-permute-start.1 = (s32[32,2]{0,1:T(2,128)S(1)}, s32[32,2]{0,1:T(2,128)S(1)}, u32[]{:S(2)}, u32[]{:S(2)}) collective-permute-start(s32[32,2]{0,1:T(2,128)S(1)} %collective-permute-done), channel_id=1, source_target_pairs={{0,384},{32,416},{64,448},{96,480},{128,0},{160,32},{192,64},{224,... | collective-permute-start | bytes 776 | tf_op jit(solution)/shard_map/ppermute | solution.py:14
  710.2 8.2 collective-permute-start.2
  718.5 4.3 collective-permute-start.3
  722.8 4.4 collective-permute-start.4
  727.2 5.2 collective-permute-start.5
  732.4 43.3 %collective-permute-start.11 = (f32[32,128,128]{2,1,0:T(8,128)}, f32[32,128,128]{2,1,0:T(8,128)}, u32[]{:S(2)}, u32[]{:S(2)}) collective-permute-start(f32[32,128,128]{2,1,0:T(8,128)} %collective-permute-done.10), channel_id=1, source_target_pairs={{0,480},{32,0},{64,32},{96,64},{128,96},{160,128},{192,160},{224,1... | collective-permute-start | bytes 6291464 | tf_op jit(solution)/shard_map/ppermute | solution.py:14
Sparse Core Ops, SparseCore 0:
  9.5 39.9 all-gather.2
  839.8 74.4 reduce-scatter.1
where the time goes:
time: 922 us; the launch traced here: 921 us
  waiting for transfers between devices  760 us (82%)
  starting transfers between devices  55.6 us (6%)
  local copies, waits for them, and re-layouts  42.5 us (5%)
  other arithmetic  18.6 us (2%)
  matrix products  17.6 us (2%)
  between operations  13.7 us (1%)
  blocking collectives  12.6 us (1%)
    ppermute x12, waiting for transfers between devices, shifted(): return lax.ppermute(value, axis, pairs)  643 us
    reduce_scatter x1, waiting for transfers between devices, shards(): return lax.psum_scatter(picked, 'layer', scatter_dimension=0, tiled=True)  74.6 us
    ppermute x12, starting transfers between devices, shifted(): return lax.ppermute(value, axis, pairs)  55.6 us
    all_gather x1, waiting for transfers between devices, shards(): lax.all_gather(blocks, 'col', axis=0, tiled=True)  42.2 us
    select_n x4, local copies, waits for them, and re-layouts, arrange(): jnp.where((row_heads >= 0)[:, None, None], shaped, jnp.float32(0.0))  23.3 us
  transfers between devices with their start and end apart: 14, of which 13 were waited for; matrix products, arithmetic and copies ran while one was open for 1% of the time, Pallas kernels for 0%

commit v1 on v0

--- a/solution.py
+++ b/solution.py
@@ -49,7 +49,9 @@
     col_index = lax.axis_index("col")
     width = blocks.shape[1]
     left_blocks, left_coords = (
-        lax.all_gather(blocks, "col", axis=0, tiled=True),
+        jnp.concatenate(
+            lax.all_to_all(jnp.stack([blocks] * lax.axis_size("col")), "col", 0, 0), axis=0
+        ),
         lax.all_gather(block_ids, "col", axis=0, tiled=True),
     )
     base_blocks, base_coords = (left_blocks, left_coords)

time: 922 us -> 905 us (0.982)
  waiting for transfers between devices: 760 us -> 614 us
  starting transfers between devices: 55.6 us -> 160 us
  blocking collectives: 12.6 us -> 41.3 us
  local copies, waits for them, and re-layouts: 42.5 us -> 30.9 us
    ppermute x12, starting transfers between devices: 55.6 us -> 160 us  [shifted(): return lax.ppermute(value, axis, pairs)]
    ppermute x12, waiting for transfers between devices: 643 us -> 548 us  [shifted(): return lax.ppermute(value, axis, pairs)]
    all_gather x1 -> x0, waiting for transfers between devices: 42.2 us -> none  [shards(): lax.all_gather(blocks, 'col', axis=0, tiled=True)]
    all_to_all x0 -> x1, blocking collectives: none -> 35.5 us  [shards(): lax.all_to_all(jnp.stack([blocks] * lax.axis_size('col')), 'col', 0, 0)]
    select_n x4 -> x2, local copies, waits for them, and re-layouts: 23.3 us -> 10.6 us  [arrange(): jnp.where((row_heads >= 0)[:, None, None], shaped, jnp.float32(0.0))]
  transfers between devices with their start and end apart: 14 -> 13, of which waited for: 13 -> 11; matrix products, arithmetic and copies ran while one was open for 1% -> 1% of each run, Pallas kernels for 0% -> 0%
where the time goes in v1:
time: 905 us; the launch traced here: 904 us
  waiting for transfers between devices  614 us (68%)
  starting transfers between devices  160 us (18%)
  blocking collectives  41.3 us (5%)
  local copies, waits for them, and re-layouts  30.9 us (3%)
  other arithmetic  26.2 us (3%)
  matrix products  17.8 us (2%)
  between operations  13.7 us (2%)
    ppermute x12, waiting for transfers between devices, shifted(): return lax.ppermute(value, axis, pairs)  548 us
    ppermute x12, starting transfers between devices, shifted(): return lax.ppermute(value, axis, pairs)  160 us
    reduce_scatter x1, waiting for transfers between devices, shards(): return lax.psum_scatter(picked, 'layer', scatter_dimension=0, tiled=True)  66.2 us
    all_to_all x1, blocking collectives, shards(): lax.all_to_all(jnp.stack([blocks] * lax.axis_size('col')), 'col', 0, 0)  35.5 us
  transfers between devices with their start and end apart: 13, of which 11 were waited for; matrix products, arithmetic and copies ran while one was open for 1% of the time, Pallas kernels for 0%

profile of v1, /device:TPU:1, one launch (start us, length us, event | category | flops | bytes accessed | tf_op | source)
XLA Modules:
  0.0 904.1 jit_solution(1556267834291571045)
XLA Ops:
  7.8 35.5 %all_to_all.5 = f32[4,8,128,128]{3,2,1,0:T(8,128)S(1)} all-to-all(f32[4,8,128,128]{3,2,1,0:T(8,128)S(1)} %stack.42), channel_id=1, replica_groups=mesh['row'=16,'col'=4,'layer'=8] {'col'}, dimensions={0} | all-to-all | bytes 4194304 | tf_op jit(solution)/shard_map/all_to_all | solution.py:53
  43.3 8.7 collective-permute-start.6
  52.0 193.6 %collective-permute-done.6 = f32[32,128,128]{2,1,0:T(8,128)S(1)} collective-permute-done((f32[32,128,128]{2,1,0:T(8,128)S(1)}, f32[32,128,128]{2,1,0:T(8,128)S(1)}, u32[]{:S(2)}, u32[]{:S(2)}) %collective-permute-start.6) | collective-permute-done | bytes 2097184 | tf_op jit(solution)/shard_map/ppermute | solution.py:14
  247.0 6.0 collective-permute-start.7
  253.0 74.3 %collective-permute-done.7 = f32[32,128,128]{2,1,0:T(8,128)} collective-permute-done((f32[32,128,128]{2,1,0:T(8,128)S(1)}, f32[32,128,128]{2,1,0:T(8,128)}, u32[]{:S(2)}, u32[]{:S(2)}) %collective-permute-start.7) | collective-permute-done | bytes 2097184 | tf_op jit(solution)/shard_map/ppermute | solution.py:14
  327.3 6.8 collective-permute-start.8
  334.1 171.8 %collective-permute-done.8 = f32[32,128,128]{2,1,0:T(8,128)} collective-permute-done((f32[32,128,128]{2,1,0:T(8,128)}, f32[32,128,128]{2,1,0:T(8,128)}, u32[]{:S(2)}, u32[]{:S(2)}) %collective-permute-start.8) | collective-permute-done | bytes 2097184 | tf_op jit(solution)/shard_map/ppermute | solution.py:14
  505.9 3.8 select_select_fusion.1
  509.7 101.8 %collective-permute-start.9 = (f32[32,128,128]{2,1,0:T(8,128)}, f32[32,128,128]{2,1,0:T(8,128)}, u32[]{:S(2)}, u32[]{:S(2)}) collective-permute-start(f32[32,128,128]{2,1,0:T(8,128)} %select_select_fusion.1), channel_id=1, source_target_pairs={{0,480},{32,0},{64,32},{96,64},{128,96},{160,128},{192,160},{224,1... | collective-permute-start | bytes 6291464 | tf_op jit(solution)/shard_map/ppermute | solution.py:14
  611.6 5.8 all-gather
  617.5 7.1 collective-permute-start
  625.0 32.0 %collective-permute-done.9 = f32[32,128,128]{2,1,0:T(8,128)} collective-permute-done((f32[32,128,128]{2,1,0:T(8,128)}, f32[32,128,128]{2,1,0:T(8,128)}, u32[]{:S(2)}, u32[]{:S(2)}) %collective-permute-start.9) | collective-permute-done | bytes 2097184 | tf_op jit(solution)/shard_map/ppermute | solution.py:14
  657.0 5.0 collective-permute-start.10
  662.8 1.9 collective-permute-start.1
  664.8 42.2 %collective-permute-done.1 = s32[32,2]{0,1:T(2,128)S(1)} collective-permute-done((s32[32,2]{0,1:T(2,128)S(1)}, s32[32,2]{0,1:T(2,128)S(1)}, u32[]{:S(2)}, u32[]{:S(2)}) %collective-permute-start.1) | collective-permute-done | bytes 288 | tf_op jit(solution)/shard_map/ppermute | solution.py:14
  707.0 7.6 collective-permute-start.2
  715.4 2.2 collective-permute-start.3
  717.6 2.0 collective-permute-done.3
  719.7 3.4 collective-permute-start.4
  724.0 4.6 collective-permute-start.5
  729.3 5.0 collective-permute-start.11
  737.0 2.0 gather_fusion.1
  739.0 3.2 select_bitcast_fusion.1
  744.1 29.8 %collective-permute-done.11 = f32[32,128,128]{2,1,0:T(8,128)} collective-permute-done((f32[32,128,128]{2,1,0:T(8,128)}, f32[32,128,128]{2,1,0:T(8,128)}, u32[]{:S(2)}, u32[]{:S(2)}) %collective-permute-start.11) | collective-permute-done | bytes 2097184 | tf_op jit(solution)/shard_map/ppermute | solution.py:14
  773.9 5.9 pad_maximum_fusion
  779.8 7.7 gather_fusion.4
  787.4 7.4 select_bitcast_fusion
  794.9 8.7 copy.33
  803.6 17.8 %fusion.10 = f32[4,128,16,128]{3,1,2,0:T(8,128)} fusion(f32[4,128,1024,1]{1,2,3,0:T(8,128)S(1)} %bitcast.73, f32[16,128,1024,1]{1,2,0,3:T(8,128)} %bitcast.68), kind=kOutput, calls=%fused_computation.61 | convolution fusion | flops 12884901888 | bytes 14680064 | tf_op jit(solution)/shard_map/dot_general | solution.py:79
  821.4 5.0 gather_fusion.2
  826.4 4.6 select_select_fusion
  831.1 66.2 %reduce-scatter.2.cloned.1.call-done = f32[8,128,128]{2,1,0:T(8,128)} async-done(((f32[64,128,128]{2,1,0:T(8,128)}), f32[8,128,128]{2,1,0:T(8,128)}) %reduce-scatter.2.cloned.1.call-update) | async-done | bytes 524304 | tf_op jit(solution)/shard_map/reduce_scatter | solution.py:95
  (56 shorter events, 10.9 us)
Async XLA Ops:
  6.5 890.7 %reduce-scatter.2.cloned.1.call-start = ((), (), s32[]{:S(2)}) async-start(), calls=%async_computation.2 | async-start | bytes 4718592 | tf_op jit(solution)/shard_map/reduce_scatter | solution.py:95
  43.3 202.3 %collective-permute-start.6 = (f32[32,128,128]{2,1,0:T(8,128)S(1)}, f32[32,128,128]{2,1,0:T(8,128)S(1)}, u32[]{:S(2)}, u32[]{:S(2)}) collective-permute-start(f32[32,128,128]{2,1,0:T(8,128)S(1)} %bitcast.70), channel_id=1, source_target_pairs={{0,384},{32,416},{64,448},{96,480},{128,0},{160,32},{192,64},{224,... | collective-permute-start | bytes 6291464 | tf_op jit(solution)/shard_map/ppermute | solution.py:14
  245.6 1.3 copy-start
  247.0 80.3 %collective-permute-start.7 = (f32[32,128,128]{2,1,0:T(8,128)S(1)}, f32[32,128,128]{2,1,0:T(8,128)}, u32[]{:S(2)}, u32[]{:S(2)}) collective-permute-start(f32[32,128,128]{2,1,0:T(8,128)S(1)} %collective-permute-done.6), channel_id=1, source_target_pairs={{0,384},{32,416},{64,448},{96,480},{128,0},{160,32},{192,64},{224,... | collective-permute-start | bytes 6291464 | tf_op jit(solution)/shard_map/ppermute | solution.py:14
  327.3 178.6 %collective-permute-start.8 = (f32[32,128,128]{2,1,0:T(8,128)}, f32[32,128,128]{2,1,0:T(8,128)}, u32[]{:S(2)}, u32[]{:S(2)}) collective-permute-start(f32[32,128,128]{2,1,0:T(8,128)} %collective-permute-done.7), channel_id=1, source_target_pairs={{0,384},{32,416},{64,448},{96,480},{128,0},{160,32},{192,64},{224,... | collective-permute-start | bytes 6291464 | tf_op jit(solution)/shard_map/ppermute | solution.py:14
  334.1 277.5 %copy-start.2 = (s32[8,2]{0,1:T(2,128)S(1)}, s32[8,2]{0,1:T(2,128)}, u32[]{:S(2)}) copy-start(s32[8,2]{0,1:T(2,128)} %param.4) | copy-start | bytes 196
  334.1 290.9 %copy-start.1 = (s32[64,2]{0,1:T(2,128)S(1)}, s32[64,2]{0,1:T(2,128)}, u32[]{:S(2)}) copy-start(s32[64,2]{0,1:T(2,128)} %param.5) | copy-start | bytes 1540
  509.7 147.3 %collective-permute-start.9 = (f32[32,128,128]{2,1,0:T(8,128)}, f32[32,128,128]{2,1,0:T(8,128)}, u32[]{:S(2)}, u32[]{:S(2)}) collective-permute-start(f32[32,128,128]{2,1,0:T(8,128)} %select_select_fusion.1), channel_id=1, source_target_pairs={{0,480},{32,0},{64,32},{96,64},{128,96},{160,128},{192,160},{224,1... | collective-permute-start | bytes 6291464 | tf_op jit(solution)/shard_map/ppermute | solution.py:14
  617.5 45.3 %collective-permute-start = (s32[32,2]{0,1:T(2,128)S(1)}, s32[32,2]{0,1:T(2,128)S(1)}, u32[]{:S(2)}, u32[]{:S(2)}) collective-permute-start(s32[32,2]{0,1:T(2,128)S(1)} %reshape.231), channel_id=1, source_target_pairs={{0,384},{32,416},{64,448},{96,480},{128,0},{160,32},{192,64},{224,... | collective-permute-start | bytes 776 | tf_op jit(solution)/shard_map/ppermute | solution.py:14
  657.0 72.3 %collective-permute-start.10 = (f32[32,128,128]{2,1,0:T(8,128)}, f32[32,128,128]{2,1,0:T(8,128)}, u32[]{:S(2)}, u32[]{:S(2)}) collective-permute-start(f32[32,128,128]{2,1,0:T(8,128)} %collective-permute-done.9), channel_id=1, source_target_pairs={{0,480},{32,0},{64,32},{96,64},{128,96},{160,128},{192,160},{224,1... | collective-permute-start | bytes 6291464 | tf_op jit(solution)/shard_map/ppermute | solution.py:14
  662.8 44.3 %collective-permute-start.1 = (s32[32,2]{0,1:T(2,128)S(1)}, s32[32,2]{0,1:T(2,128)S(1)}, u32[]{:S(2)}, u32[]{:S(2)}) collective-permute-start(s32[32,2]{0,1:T(2,128)S(1)} %collective-permute-done), channel_id=1, source_target_pairs={{0,384},{32,416},{64,448},{96,480},{128,0},{160,32},{192,64},{224,... | collective-permute-start | bytes 776 | tf_op jit(solution)/shard_map/ppermute | solution.py:14
  707.0 8.3 collective-permute-start.2
  715.4 4.3 collective-permute-start.3
  719.7 4.3 collective-permute-start.4
  724.0 5.3 collective-permute-start.5
  729.3 44.6 %collective-permute-start.11 = (f32[32,128,128]{2,1,0:T(8,128)}, f32[32,128,128]{2,1,0:T(8,128)}, u32[]{:S(2)}, u32[]{:S(2)}) collective-permute-start(f32[32,128,128]{2,1,0:T(8,128)} %collective-permute-done.10), channel_id=1, source_target_pairs={{0,480},{32,0},{64,32},{96,64},{128,96},{160,128},{192,160},{224,1... | collective-permute-start | bytes 6291464 | tf_op jit(solution)/shard_map/ppermute | solution.py:14
Sparse Core Ops, SparseCore 0:
  831.2 65.9 reduce-scatter.1
